TPU v7x, 256 devices: a whole 4x4x8 slice. The times are simulated.
256 devices in a mesh: op: 64 (over y, z_hi, x, core), sec: 4 (over z_lo).
Axes of the slice: x: 4, y: 4, z: 8 (z_hi: 2, z_lo: 4; z = z_hi * 4 + z_lo), core: 2. Of those that a mesh axis runs over, the one named last changes fastest.
Arguments:
- wavefunction: bfloat16 [16, 256, 256], P('sec'), may hold values from -6 to 6
- left_operators: bfloat16 [256, 16, 256, 256], P('op', 'sec'), may hold values from -0.375 to 0.375
- right_operators: bfloat16 [256, 16, 256, 256], P('op', 'sec'), may hold values from -0.375 to 0.375
- rotations: bfloat16 [16, 256, 256], P('sec'), may hold values from -0.375 to 0.375
- charges: int32 [256], P('op'), may hold values from -1 to 1
- present_blocks: int32 [256, 16], P('op', 'sec'), may hold values 0 or 1
- directions: int32 [256, 1], P('op'), may hold values from 0 to 3, as said below
Outputs:
- sigma_vector: float32 [16, 256, 256], P('sec', 'op')
- regrouped: bfloat16 [512, 16, 256, 256], P('op', 'sec')
Inputs may be any that keep to these rules, and one draw needn't show every extreme that they name: `directions`: among the pairs of one index of op, each direction is named by at most 2 pairs, some direction is named by exactly 2, and every direction other than 0 is named at least once.
All inputs are finite; a program needn't handle non-finite values. No bound on the sum of `present_blocks` on one device may be relied on, other than what follows from the above.
Results may differ from a plain program's by a relative error of at most 0.0049.
Values may be sent and summed in bfloat16 or wider, within the bound.
A program may use at most 64 MiB of HBM per device.

v0:
```python
import math

import jax
import jax.numpy as jnp
from jax import lax
from jax.sharding import PartitionSpec as P

DIRS = 4
CAPS = 2


def passed_along(value, axis, steps):
    count = lax.axis_size(axis)
    leading, last = (max(0, -steps), min(count, count - steps))
    return lax.ppermute(value, axis, [(source, source + steps) for source in range(leading, last)])


def padded(cells, sides, width):
    for axis, dim in sides:
        count = lax.axis_size(axis)
        ends = count - 1
        head = lax.slice_in_dim(cells, 0, width, axis=dim)
        tail = lax.slice_in_dim(cells, cells.shape[dim] - width, cells.shape[dim], axis=dim)
        cells = jnp.concatenate(
            [
                lax.ppermute(tail, axis, [(i, (i + 1) % count) for i in range(ends)]),
                cells,
                lax.ppermute(head, axis, [((i + 1) % count, i) for i in range(ends)]),
            ],
            axis=dim,
        )
    return cells


def shifted(value, axis, by):
    devices = lax.axis_size(axis)
    return lax.ppermute(value, axis, [(i, (i + by) % devices) for i in range(devices)])


def body(
    wavefunction, left_operators, right_operators, rotations, charges, present_blocks, directions
):
    local_sectors = wavefunction.shape[0]
    local_pairs = left_operators.shape[0]
    width = wavefunction.shape[1]
    weights = present_blocks.astype(jnp.float32)
    halfway = jnp.einsum(
        "psij,sjk->psik", left_operators, wavefunction, preferred_element_type=jnp.float32
    ).astype(jnp.bfloat16)
    charge_values = jnp.arange(3, dtype=jnp.int32) - 1
    selector = (charges[None, :] == charge_values[:, None]).astype(jnp.bfloat16)[
        :, :, None
    ] * present_blocks.astype(jnp.bfloat16)[None, :, :]
    masked = selector[:, :, :, None, None] * halfway[None]
    partials = jnp.einsum(
        "cpsik,psmk->csim", masked, right_operators, preferred_element_type=jnp.float32
    )
    padding = jnp.zeros((1, width, width), jnp.float32)
    extended = (
        jnp.concatenate([partials[0], padding, padding], axis=0)
        + jnp.concatenate([padding, partials[1], padding], axis=0)
        + jnp.concatenate([padding, padding, partials[2]], axis=0)
    )
    from_below = passed_along(extended[local_sectors + 1].astype(jnp.bfloat16), "sec", 1).astype(
        jnp.float32
    )
    from_above = passed_along(extended[0].astype(jnp.bfloat16), "sec", -1).astype(jnp.float32)
    interior = extended[1 : local_sectors + 1]
    interior = interior.at[0].add(from_below).at[local_sectors - 1].add(from_above)
    summed = lax.psum_scatter(interior, "op", scatter_dimension=1, tiled=True)
    pair_total = local_pairs * lax.axis_size("op")
    sigma_vector = summed / math.sqrt(pair_total)
    rot_padded = padded(rotations, (("sec", 0),), 1)
    rotated = jnp.einsum(
        "psij,sjk->psik", left_operators, rotations, preferred_element_type=jnp.float32
    ).astype(jnp.bfloat16)
    indices = jnp.arange(local_sectors, dtype=jnp.int32)[None, :] + 1 + charges[:, None]
    target = rot_padded[indices]
    renormed = (
        jnp.einsum("psji,psjk->psik", target, rotated, preferred_element_type=jnp.float32)
        * weights[:, :, None, None]
    ).astype(jnp.bfloat16)
    kinds = directions[:, 0]
    matching = kinds[:, None] == kinds[None, :]
    earlier = jnp.arange(local_pairs)[None, :] < jnp.arange(local_pairs)[:, None]
    position = jnp.sum(jnp.logical_and(matching, earlier), axis=1)
    chooser = jnp.logical_and(
        kinds[None, None, :] == jnp.arange(DIRS)[:, None, None],
        position[None, None, :] == jnp.arange(CAPS)[None, :, None],
    ).astype(jnp.bfloat16)
    payload = jnp.einsum(
        "dcp,psik->dcsik", chooser, renormed, preferred_element_type=jnp.float32
    ).astype(jnp.bfloat16)
    half_axis = lax.axis_size("op") // 2
    moved_one = shifted(payload[1], "op", 1)
    moved_two = shifted(payload[2], "op", -1)
    moved_three = shifted(payload[3], "op", half_axis)
    regrouped = jnp.stack([payload[0], moved_one, moved_two, moved_three], axis=0)
    regrouped = regrouped.reshape(DIRS * CAPS, local_sectors, width, width)
    return (sigma_vector, regrouped)


def solution(mesh):
    placed = (
        P("sec", None, None),
        P("op", "sec", None, None),
        P("op", "sec", None, None),
        P("sec", None, None),
        P("op"),
        P("op", "sec"),
        P("op", None),
    )
    return jax.shard_map(
        body,
        mesh=mesh,
        in_specs=placed,
        out_specs=(P("sec", "op", None), P("op", "sec", None, None)),
        check_vma=False,
    )
```

profile of v0, /device:TPU:1, one launch (start us, length us, event | category | flops | bytes accessed | tf_op | source)
XLA Modules:
  0.0 888.0 jit_solution(14384372589298855152)
XLA Ops:
  8.4 4.4 collective-permute-start.2
  12.7 1.3 collective-permute-start.3
  18.0 3.2 convert_bitcast_fusion
  21.2 2.1 convert_bitcast_fusion.1
  23.3 4.2 copy.68
  27.4 4.1 fusion.8
  31.7 1.8 fusion.25
  34.6 2.0 gather_fusion
  36.6 3.1 multiply_convert_fusion
  39.8 2.5 convolution_convert_fusion
  42.3 7.1 fusion.27
  52.9 2.0 collective-permute-start.4
  54.9 2.9 collective-permute-start.6
  58.8 4.3 collective-permute-start
  63.1 1.3 collective-permute-start.1
  65.1 5.7 collective-permute-done.1
  73.1 3.0 copy.77
  76.1 3.0 copy.78
  79.1 9.7 %collective-permute-done.6 = bf16[2,4,256,256]{3,2,1,0:T(8,128)(2,1)} collective-permute-done((bf16[2,4,256,256]{3,2,1,0:T(8,128)(2,1)}, bf16[2,4,256,256]{3,2,1,0:T(8,128)(2,1)}, u32[]{:S(2)}, u32[]{:S(2)}) %collective-permute-start.6) | collective-permute-done | bytes 1048608 | tf_op jit(solution)/shard_map/ppermute | solution.py:37
  88.8 3.0 copy.79
  91.8 9.8 %pad_maximum_fusion = bf16[4,2,4,256,256]{4,0,3,2,1:T(4,128)(2,1)S(1)} fusion(bf16[1,2,4,256,256]{4,0,3,2,1:T(2,128)(2,1)S(1)} %copy.79, bf16[1,2,4,256,256]{4,0,3,2,1:T(2,128)(2,1)S(1)} %copy.78, bf16[1,2,4,256,256]{4,0,3,2,1:T(2,128)(2,1)S(1)} %copy.77, bf16[1,2,4,256,256]{4,0,3,2,1:T(2,128)(2,1)S(1)} %copy-done.1), kind=kLoop, calls=%fused_computation.3 | loop fusion | flops 16777216 | bytes 8388608 | tf_op jit(solution)/shard_map/stack | solution.py:98
  101.6 2.8 copy.80
  104.4 775.4 %all-reduce.5.cloned.1.call-done = f32[4,256,256]{2,1,0:T(8,128)} async-done(((f32[4,256,256]{2,1,0:T(8,128)}), f32[4,256,256]{2,1,0:T(8,128)}) %all-reduce.5.cloned.1.call-update) | async-done | bytes 1048592
  879.8 1.4 dynamic-slice_multiply_fusion
  (46 shorter events, 13.2 us)
Async XLA Ops:
  7.2 10.8 %copy-start = (bf16[4,4,256,256]{3,2,1,0:T(8,128)(2,1)S(1)}, bf16[4,4,256,256]{3,2,1,0:T(8,128)(2,1)}, u32[]{:S(2)}) copy-start(bf16[4,4,256,256]{3,2,1,0:T(8,128)(2,1)} %param.12) | copy-start | bytes 6291460
  7.2 872.7 %all-reduce.5.cloned.1.call-start = ((), (), s32[]{:S(2)}) async-start(), calls=%async_computation | async-start | bytes 2097152
  8.4 25.2 %collective-permute-start.2 = (bf16[1,256,256]{2,1,0:T(8,128)(2,1)S(1)}, bf16[1,256,256]{2,1,0:T(8,128)(2,1)S(1)}, u32[]{:S(2)}, u32[]{:S(2)}) collective-permute-start(bf16[1,256,256]{2,1,0:T(8,128)(2,1)S(1)} %get-tuple-element.37), channel_id=1, source_target_pairs={{0,1},{1,2},{2,3},{4,5},{5,6},{6,7},{8,9},{9,10},{10,11},{12,13},{... | collective-permute-start | bytes 393224 | tf_op jit(solution)/shard_map/ppermute | solution.py:26
  12.7 20.9 %collective-permute-start.3 = (bf16[1,256,256]{2,1,0:T(8,128)(2,1)S(1)}, bf16[1,256,256]{2,1,0:T(8,128)(2,1)}, u32[]{:S(2)}, u32[]{:S(2)}) collective-permute-start(bf16[1,256,256]{2,1,0:T(8,128)(2,1)S(1)} %get-tuple-element.38), channel_id=1, source_target_pairs={{1,0},{2,1},{3,2},{5,4},{6,5},{7,6},{9,8},{10,9},{11,10},{13,12},{... | collective-permute-start | bytes 393224 | tf_op jit(solution)/shard_map/ppermute | solution.py:28
  18.0 3.2 copy-start.5
  31.7 1.9 copy-start.4
  51.7 12.7 %copy-start.3 = (f32[6,256,256]{2,1,0:T(8,128)S(1)}, f32[6,256,256]{2,1,0:T(8,128)}, u32[]{:S(2)}) copy-start(f32[6,256,256]{2,1,0:T(8,128)} %get-tuple-element.27) | copy-start | bytes 4718596
  52.9 20.2 %collective-permute-start.4 = (bf16[2,4,256,256]{3,2,1,0:T(8,128)(2,1)}, bf16[2,4,256,256]{3,2,1,0:T(8,128)(2,1)}, u32[]{:S(2)}, u32[]{:S(2)}) collective-permute-start(bf16[2,4,256,256]{3,2,1,0:T(8,128)(2,1)} %bitcast.71), channel_id=1, source_target_pairs={{0,4},{4,8},{8,12},{12,16},{16,20},{20,24},{24,28},{28,32},{32,36}... | collective-permute-start | bytes 3145736 | tf_op jit(solution)/shard_map/ppermute | solution.py:37
  54.9 21.2 %collective-permute-start.5 = (bf16[2,4,256,256]{3,2,1,0:T(8,128)(2,1)}, bf16[2,4,256,256]{3,2,1,0:T(8,128)(2,1)}, u32[]{:S(2)}, u32[]{:S(2)}) collective-permute-start(bf16[2,4,256,256]{3,2,1,0:T(8,128)(2,1)} %bitcast.70), channel_id=1, source_target_pairs={{0,252},{4,0},{8,4},{12,8},{16,12},{20,16},{24,20},{28,24},{32,28}... | collective-permute-start | bytes 3145736 | tf_op jit(solution)/shard_map/ppermute | solution.py:37
  54.9 33.9 %collective-permute-start.6 = (bf16[2,4,256,256]{3,2,1,0:T(8,128)(2,1)}, bf16[2,4,256,256]{3,2,1,0:T(8,128)(2,1)}, u32[]{:S(2)}, u32[]{:S(2)}) collective-permute-start(bf16[2,4,256,256]{3,2,1,0:T(8,128)(2,1)} %bitcast.69), channel_id=1, source_target_pairs={{0,128},{4,132},{8,136},{12,140},{16,144},{20,148},{24,152},{28,15... | collective-permute-start | bytes 3145736 | tf_op jit(solution)/shard_map/ppermute | solution.py:37
  58.8 6.2 collective-permute-start
  63.1 7.7 collective-permute-start.1
  64.4 7.4 copy-start.6
  70.8 1.0 copy-start.2
  79.1 12.7 %copy-start.1 = (bf16[1,2,4,256,256]{4,0,3,2,1:T(2,128)(2,1)S(1)}, bf16[1,2,4,256,256]{4,0,3,2,1:T(2,128)(2,1)}, u32[]{:S(2)}) copy-start(bf16[1,2,4,256,256]{4,0,3,2,1:T(2,128)(2,1)} %get-tuple-element.28) | copy-start | bytes 3145732
Sparse Core Ops, SparseCore 0:
  72.0 807.8 all-reduce.4
where the time goes:
time: 889 us; the launch traced here: 888 us
  waiting for transfers between devices  791 us (89%)
  local copies, waits for them, and re-layouts  32.6 us (4%)
  other arithmetic  17.8 us (2%)
  starting transfers between devices  16.2 us (2%)
  matrix products  15 us (2%)
  between operations  14.9 us (2%)
    unnamed x2, waiting for transfers between devices  775 us
  transfers between devices with their start and end apart: 8, of which 4 were waited for; matrix products, arithmetic and copies ran while one was open for 5% of the time, Pallas kernels for 0%

commit v1 on v0

v1 whole, which is shorter than its diff:
```python
import jax
import jax.numpy as jnp
from jax import lax
from jax.experimental import pallas as pl
from jax.experimental.pallas import tpu as pltpu
from jax.sharding import PartitionSpec as P

MESH = pl.DeviceIdType.MESH
F32 = jnp.float32
BF16 = jnp.bfloat16
NT = (((1,), (1,)), ((), ()))


def place(y, zh, x, c):
    return y * 16 + zh * 8 + x * 2 + c


def kernel(
    chg, pres, dirs, psi_h, left_h, right_h, rot_h,
    sig, reg,
    psi, left, right, rot, rot_t, rot_in, half, rotd, pay, zero_blk,
    part, c_in, x_out, x_in, f2, y_out, y_in, z_out, z_in, e_out, e_in,
    in_sem, rot_s, rot_r, pay_s, pay_r, loc_sem, c_s, c_r, x_s, x_r, y_s, y_r, z_s, z_r, e_s, e_r,
):
    d = lax.axis_index("op")
    s = lax.axis_index("sec")
    y, zh, x, c = d // 16, (d // 8) % 2, (d // 2) % 4, d % 2
    core_peer = place(y, zh, x, 1 - c)
    x_peer = [place(y, zh, (x + o) % 4, c) for o in (1, 2, 3)]
    y_peer = [place((y + o) % 4, zh, x, c) for o in (1, 2, 3)]
    zh_peer = place(y, 1 - zh, x, c)
    up, down, across = (d + 1) % 64, (d + 63) % 64, (d + 32) % 64

    loads = [
        pltpu.make_async_copy(rot_h, rot, in_sem.at[0]),
        pltpu.make_async_copy(psi_h, psi, in_sem.at[1]),
    ]
    for p in range(4):
        loads.append(pltpu.make_async_copy(left_h.at[pl.ds(4 * p, 4)], left.at[pl.ds(4 * p, 4)], in_sem.at[2 + p]))
    loads.append(pltpu.make_async_copy(right_h, right, in_sem.at[6]))

    bar = pltpu.get_barrier_semaphore()
    for peer in [core_peer, zh_peer, up, down] + x_peer + y_peer:
        pl.semaphore_signal(bar, inc=1, device_id=(peer, s), device_id_type=MESH)

    @pl.when(s > 0)
    def _():
        for peer in (d, zh_peer):
            pl.semaphore_signal(bar, inc=1, device_id=(peer, s - 1), device_id_type=MESH)

    @pl.when(s < 3)
    def _():
        for peer in (d, zh_peer):
            pl.semaphore_signal(bar, inc=1, device_id=(peer, s + 1), device_id_type=MESH)

    for copy in loads:
        copy.start()
    sides = jnp.where(s > 0, 2, 0) + jnp.where(s < 3, 2, 0)
    pl.semaphore_wait(bar, 10 + sides)

    loads[0].wait()

    def to_above():
        return pltpu.make_async_remote_copy(
            rot.at[3], rot_in.at[0], rot_s.at[0], rot_r.at[0], device_id=(d, s + 1), device_id_type=MESH)

    def to_below():
        return pltpu.make_async_remote_copy(
            rot.at[0], rot_in.at[1], rot_s.at[1], rot_r.at[1], device_id=(d, s - 1), device_id_type=MESH)

    @pl.when(s < 3)
    def _():
        to_above().start()

    @pl.when(s > 0)
    def _():
        to_below().start()

    zero_blk[...] = jnp.zeros_like(zero_blk)
    half[16] = jnp.zeros((256, 256), BF16)

    def flip(i, _):
        rot_t[i + 1] = rot[i].T
        return 0

    lax.fori_loop(0, 4, flip, 0)

    loads[1].wait()
    for p in range(4):
        loads[2 + p].wait()

        def stage_one(i, _, p=p):
            block = left[4 * p + i]
            w = pres[p, i].astype(F32)
            half[4 * p + i] = (jnp.dot(block, psi[i], preferred_element_type=F32) * w).astype(BF16)
            rotd[4 * p + i] = jnp.dot(block, rot[i], preferred_element_type=F32).astype(BF16)
            return 0

        lax.fori_loop(0, 4, stage_one, 0)

    kinds = [dirs[p, 0] for p in range(4)]
    fresh = []
    for p in range(4):
        seen = jnp.int32(0)
        for q in range(p):
            seen = seen + (kinds[q] == kinds[p]).astype(jnp.int32)
        fresh.append((seen == 0).astype(jnp.int32))
    first = {}
    for k in (1, 2, 3):
        pick = jnp.int32(0)
        for p in range(1, 4):
            pick = pick + p * fresh[p] * (kinds[p] == k).astype(jnp.int32)
        first[k] = pick
    extra = 6 - first[1] - first[2] - first[3]
    extra = jnp.clip(extra, 0, 3)
    extra_kind = dirs[extra, 0]

    @pl.when(s > 0)
    def _():
        to_above().wait_recv()
        rot_t[0] = rot_in[0].T

    @pl.when(s == 0)
    def _():
        rot_t[0] = jnp.zeros((256, 256), BF16)

    @pl.when(s < 3)
    def _():
        to_below().wait_recv()
        rot_t[5] = rot_in[1].T

    @pl.when(s == 3)
    def _():
        rot_t[5] = jnp.zeros((256, 256), BF16)

    def moved(k, j):
        to = {1: up, 2: down, 3: across}[k]
        n = 2 * (k - 1) + j
        return pltpu.make_async_remote_copy(
            pay.at[n], reg.at[2 * k + j], pay_s.at[n], pay_r.at[n], device_id=(to, s), device_id_type=MESH)

    def renormed(p, i):
        w = pres[p, i].astype(F32)
        return jnp.dot(rot_t[i + 1 + chg[p]], rotd[4 * p + i], preferred_element_type=F32) * w

    for k in (3, 1, 2):
        pair = first[k]

        def stage_two(i, _, pair=pair, k=k):
            pay[2 * (k - 1), i] = renormed(pair, i).astype(BF16)
            return 0

        lax.fori_loop(0, 4, stage_two, 0)
        moved(k, 0).start()

    def stage_three(i, _):
        block = renormed(extra, i)
        for k in (3, 1, 2):
            pay[2 * (k - 1) + 1, i] = (block * (extra_kind == k).astype(F32)).astype(BF16)
        pay[6, i] = (block * (extra_kind == 0).astype(F32)).astype(BF16)
        return 0

    lax.fori_loop(0, 4, stage_three, 0)
    for k in (3, 1, 2):
        moved(k, 1).start()
    stay = pltpu.make_async_copy(pay.at[6], reg.at[0], loc_sem.at[0])
    blank = pltpu.make_async_copy(zero_blk, reg.at[1], loc_sem.at[1])
    stay.start()
    blank.start()

    loads[6].wait()
    row = lax.broadcasted_iota(jnp.int32, (256, 256), 0)
    col = lax.broadcasted_iota(jnp.int32, (256, 256), 1)
    natural = ((row // 8) % 4) * 64 + ((row // 4) % 2) * 32 + ((row // 32) % 4) * 8 + (row // 128) * 4 + row % 4
    order = (col == natural).astype(BF16)

    def target_sum(e, _):
        total = jnp.zeros((256, 256), F32)
        for p in range(4):
            src = e - 1 - chg[p]
            inside = jnp.logical_and(src >= 0, src <= 3)
            clipped = jnp.clip(src, 0, 3)
            lhs = half[jnp.where(inside, 4 * p + clipped, 16)]
            total = total + lax.dot_general(lhs, right[4 * p + clipped], NT, preferred_element_type=F32)
        placed = jnp.dot(order, total.astype(BF16), preferred_element_type=F32).astype(BF16)
        part[e, 0] = placed[:128]
        part[e, 1] = placed[128:]
        return 0

    lax.fori_loop(0, 6, target_sum, 0)

    to_core = pltpu.make_async_remote_copy(
        part.at[:, 1 - c], c_in, c_s.at[0], c_r.at[0], device_id=(core_peer, s), device_id_type=MESH)
    to_core.start()
    to_core.wait()

    def core_sum(e, _):
        both = part[e, c].astype(F32) + c_in[e].astype(F32)
        x_out[e] = both.reshape(4, 32, 256).astype(BF16)
        return 0

    lax.fori_loop(0, 6, core_sum, 0)
    to_x = []
    for o in range(3):
        copy = pltpu.make_async_remote_copy(
            x_out.at[:, (x + o + 1) % 4], x_in.at[o], x_s.at[o], x_r.at[o],
            device_id=(x_peer[o], s), device_id_type=MESH)
        copy.start()
        to_x.append(copy)
    for copy in to_x:
        copy.wait()
    rows = pl.ds(pl.multiple_of(x * 32, 32), 32)

    def x_sum(e, _):
        total = part[e, c, rows].astype(F32) + c_in[e, rows].astype(F32)
        for o in range(3):
            total = total + x_in[o, e].astype(F32)
        for q in range(4):
            f2[q, e] = total[8 * q:8 * q + 8]
        return 0

    lax.fori_loop(0, 6, x_sum, 0)
    for q in range(4):
        y_out[q] = f2[q].reshape(48, 256).astype(BF16)
    to_y = []
    for o in range(3):
        copy = pltpu.make_async_remote_copy(
            y_out.at[(y + o + 1) % 4], y_in.at[o], y_s.at[o], y_r.at[o],
            device_id=(y_peer[o], s), device_id_type=MESH)
        copy.start()
        to_y.append(copy)
    for copy in to_y:
        copy.wait()
    total = f2[y].reshape(48, 256)
    for o in range(3):
        total = total + y_in[o].astype(F32)
    z_out[...] = total[8:40].astype(BF16)
    e_out[0] = total[0:8]
    e_out[1] = total[40:48]
    to_z = pltpu.make_async_remote_copy(
        z_out, z_in, z_s.at[0], z_r.at[0], device_id=(zh_peer, s), device_id_type=MESH)
    to_z.start()

    def edge(side, far):
        op_to = zh_peer if far else d
        sec_to = s + 1 if side else s - 1
        return pltpu.make_async_remote_copy(
            e_out.at[side], e_in.at[side, far], e_s.at[side, far], e_r.at[side, far],
            device_id=(op_to, sec_to), device_id_type=MESH)

    @pl.when(s < 3)
    def _():
        edge(1, 0).start()
        edge(1, 1).start()

    @pl.when(s > 0)
    def _():
        edge(0, 0).start()
        edge(0, 1).start()

    to_z.wait()
    mine = (total[8:40] + z_in[...].astype(F32)).reshape(4, 8, 256)
    f2[0, pl.ds(0, 4)] = mine

    @pl.when(s > 0)
    def _():
        edge(1, 0).wait_recv()
        edge(1, 1).wait_recv()
        f2[0, 0] = f2[0, 0] + e_in[1, 0] + e_in[1, 1]

    @pl.when(s < 3)
    def _():
        edge(0, 0).wait_recv()
        edge(0, 1).wait_recv()
        f2[0, 3] = f2[0, 3] + e_in[0, 0] + e_in[0, 1]

    final = f2[0, pl.ds(0, 4)] * (1.0 / 16.0)
    sig[...] = jnp.where(zh == 0, final[:, 0:4], final[:, 4:8])

    @pl.when(s < 3)
    def _():
        edge(1, 0).wait_send()
        edge(1, 1).wait_send()
        to_above().wait_send()

    @pl.when(s > 0)
    def _():
        edge(0, 0).wait_send()
        edge(0, 1).wait_send()
        to_below().wait_send()

    for k in (3, 1, 2):
        for j in (0, 1):
            moved(k, j).wait()
    stay.wait()
    blank.wait()


def body(wavefunction, left_operators, right_operators, rotations, charges, present_blocks, directions):
    hbm = pl.BlockSpec(memory_space=pltpu.HBM)
    smem = pl.BlockSpec(memory_space=pltpu.SMEM)
    dma = pltpu.SemaphoreType.DMA
    sigma, regrouped = pl.pallas_call(
        kernel,
        out_shape=(
            jax.ShapeDtypeStruct((4, 4, 256), F32),
            jax.ShapeDtypeStruct((8, 4, 256, 256), BF16),
        ),
        in_specs=[smem, smem, smem, hbm, hbm, hbm, hbm],
        out_specs=(pl.BlockSpec(memory_space=pltpu.VMEM), hbm),
        scratch_shapes=[
            pltpu.VMEM((4, 256, 256), BF16),
            pltpu.VMEM((16, 256, 256), BF16),
            pltpu.VMEM((16, 256, 256), BF16),
            pltpu.VMEM((4, 256, 256), BF16),
            pltpu.VMEM((6, 256, 256), BF16),
            pltpu.VMEM((2, 256, 256), BF16),
            pltpu.VMEM((17, 256, 256), BF16),
            pltpu.VMEM((16, 256, 256), BF16),
            pltpu.VMEM((7, 4, 256, 256), BF16),
            pltpu.VMEM((4, 256, 256), BF16),
            pltpu.VMEM((6, 2, 128, 256), BF16),
            pltpu.VMEM((6, 128, 256), BF16),
            pltpu.VMEM((6, 4, 32, 256), BF16),
            pltpu.VMEM((3, 6, 32, 256), BF16),
            pltpu.VMEM((4, 6, 8, 256), F32),
            pltpu.VMEM((4, 48, 256), BF16),
            pltpu.VMEM((3, 48, 256), BF16),
            pltpu.VMEM((32, 256), BF16),
            pltpu.VMEM((32, 256), BF16),
            pltpu.VMEM((2, 8, 256), F32),
            pltpu.VMEM((2, 2, 8, 256), F32),
            dma((7,)), dma((2,)), dma((2,)), dma((6,)), dma((6,)), dma((2,)),
            dma((1,)), dma((1,)), dma((3,)), dma((3,)), dma((3,)), dma((3,)),
            dma((1,)), dma((1,)), dma((2, 2)), dma((2, 2)),
        ],
        compiler_params=pltpu.CompilerParams(
            collective_id=0, has_side_effects=True, vmem_limit_bytes=48 * 1024 * 1024),
        name="step",
    )(
        charges, present_blocks, directions,
        wavefunction,
        left_operators.reshape(16, 256, 256),
        right_operators.reshape(16, 256, 256),
        rotations,
    )
    return sigma, regrouped


def solution(mesh):
    placed = (
        P("sec", None, None),
        P("op", "sec", None, None),
        P("op", "sec", None, None),
        P("sec", None, None),
        P("op"),
        P("op", "sec"),
        P("op", None),
    )
    return jax.shard_map(
        body,
        mesh=mesh,
        in_specs=placed,
        out_specs=(P("sec", "op", None), P("op", "sec", None, None)),
        check_vma=False,
    )
```

time: 889 us -> 72.3 us (0.08)
  the two profiles are of different devices: /device:TPU:1 before, /device:TPU:6 now
where the time goes in v1:
time: 72.3 us; the launch traced here: 71.9 us
  Pallas kernels  58.7 us (81%)
  local copies, waits for them, and re-layouts  12.6 us (17%)
    pallas_call x1, Pallas kernels, body(): pl.pallas_call(kernel, out_shape=(jax.ShapeDtypeStruct((4, 4, 256), F32),...  58.7 us
    unnamed x15, local copies, waits for them, and re-layouts  12.6 us

profile of v1, /device:TPU:6, one launch (start us, length us, event | category | flops | bytes accessed | tf_op | source)
XLA Modules:
  0.0 71.9 jit_solution(13245670154455734359)
XLA Ops:
  0.6 0.7 %copy.9.dirs = s32[4,1]{1,0:T(4,128)S(1)} copy(s32[4,1]{0,1:T(1,128)} %param.13) | data formatting | bytes 32 | tf_op args[6]
  1.4 0.0 copy-start
  1.4 1.6 %copy-done = bf16[4,4,256,256]{3,2,1,0:T(8,128)(2,1)S(1)} copy-done((bf16[4,4,256,256]{3,2,1,0:T(8,128)(2,1)S(1)}, bf16[4,4,256,256]{3,2,1,0:T(8,128)(2,1)}, u32[]{:S(2)}) %copy-start) | copy-done | bytes 2097176
  3.0 0.0 copy-start.1
  3.0 1.6 %copy-done.1 = bf16[4,4,256,256]{3,2,1,0:T(8,128)(2,1)S(1)} copy-done((bf16[4,4,256,256]{3,2,1,0:T(8,128)(2,1)S(1)}, bf16[4,4,256,256]{3,2,1,0:T(8,128)(2,1)}, u32[]{:S(2)}) %copy-start.1) | copy-done | bytes 2097176
  4.6 0.0 copy-start.2
  4.6 1.0 %copy-done.2 = bf16[4,256,256]{2,1,0:T(8,128)(2,1)S(1)} copy-done((bf16[4,256,256]{2,1,0:T(8,128)(2,1)S(1)}, bf16[4,256,256]{2,1,0:T(8,128)(2,1)}, u32[]{:S(2)}) %copy-start.2) | copy-done | bytes 524312
  5.6 0.0 copy-start.3
  5.6 1.0 %copy-done.3 = bf16[4,256,256]{2,1,0:T(8,128)(2,1)S(1)} copy-done((bf16[4,256,256]{2,1,0:T(8,128)(2,1)S(1)}, bf16[4,256,256]{2,1,0:T(8,128)(2,1)}, u32[]{:S(2)}) %copy-start.3) | copy-done | bytes 524312
  6.6 0.0 copy-start.4
  6.6 0.7 copy-done.4
  7.3 0.0 copy-start.5
  7.3 0.7 copy-done.5
  8.0 58.7 %step.1 = (f32[4,4,256]{2,1,0:T(4,128)S(1)}, bf16[8,4,256,256]{3,2,1,0:T(8,128)(2,1)}) custom-call(s32[4]{0:T(128)S(1)} %copy-done.5, s32[4,4]{1,0:T(4,128)S(1)} %copy-done.4, s32[4,1]{1,0:T(4,128)S(1)} %copy.9.dirs, bf16[4,256,256]{2,1,0:T(8,128)(2,1)S(1)} %copy-done.2, bf16[16,256,256]{2,1,0:T(8,128)(2,1)S(1)} %bitcast.2, ...), custom_call_target="tpu_custom_call" | custom-call | tf_op jit(solution)/shard_map/step/pallas_call | solution.py:303
  66.7 0.6 copy.12
  67.3 4.6 %copy.13 = bf16[8,4,256,256]{3,2,1,0:T(8,128)(2,1)} copy(bf16[8,4,256,256]{3,2,1,0:T(8,128)(2,1)} %get-tuple-element.5) | data formatting | bytes 8388608
Async XLA Ops:
  1.4 1.6 %copy-start = (bf16[4,4,256,256]{3,2,1,0:T(8,128)(2,1)S(1)}, bf16[4,4,256,256]{3,2,1,0:T(8,128)(2,1)}, u32[]{:S(2)}) copy-start(bf16[4,4,256,256]{3,2,1,0:T(8,128)(2,1)} %param.8) | copy-start | bytes 6291460
  3.0 1.6 %copy-start.1 = (bf16[4,4,256,256]{3,2,1,0:T(8,128)(2,1)S(1)}, bf16[4,4,256,256]{3,2,1,0:T(8,128)(2,1)}, u32[]{:S(2)}) copy-start(bf16[4,4,256,256]{3,2,1,0:T(8,128)(2,1)} %param.9) | copy-start | bytes 6291460
  4.6 1.0 %copy-start.2 = (bf16[4,256,256]{2,1,0:T(8,128)(2,1)S(1)}, bf16[4,256,256]{2,1,0:T(8,128)(2,1)}, u32[]{:S(2)}) copy-start(bf16[4,256,256]{2,1,0:T(8,128)(2,1)} %psi_h.1) | copy-start | bytes 1572868
  5.6 1.0 %copy-start.3 = (bf16[4,256,256]{2,1,0:T(8,128)(2,1)S(1)}, bf16[4,256,256]{2,1,0:T(8,128)(2,1)}, u32[]{:S(2)}) copy-start(bf16[4,256,256]{2,1,0:T(8,128)(2,1)} %rot_h.1) | copy-start | bytes 1572868
  6.6 0.7 copy-start.4
  7.3 0.7 copy-start.5

commit v2 on v1

--- a/solution.py
+++ b/solution.py
@@ -18,9 +18,9 @@
 def kernel(
     chg, pres, dirs, psi_h, left_h, right_h, rot_h,
     sig, reg,
-    psi, left, right, rot, rot_t, rot_in, half, rotd, pay, zero_blk,
+    psi, left, right, rot, rot_t, rot_in, half, rotd, pay,
     part, c_in, x_out, x_in, f2, y_out, y_in, z_out, z_in, e_out, e_in,
-    in_sem, rot_s, rot_r, pay_s, pay_r, loc_sem, c_s, c_r, x_s, x_r, y_s, y_r, z_s, z_r, e_s, e_r,
+    in_sem, rot_s, rot_r, pay_s, pay_r, c_s, c_r, x_s, x_r, y_s, y_r, z_s, z_r, e_s, e_r,
 ):
     d = lax.axis_index("op")
     s = lax.axis_index("sec")
@@ -55,28 +55,7 @@
 
     for copy in loads:
         copy.start()
-    sides = jnp.where(s > 0, 2, 0) + jnp.where(s < 3, 2, 0)
-    pl.semaphore_wait(bar, 10 + sides)
-
     loads[0].wait()
-
-    def to_above():
-        return pltpu.make_async_remote_copy(
-            rot.at[3], rot_in.at[0], rot_s.at[0], rot_r.at[0], device_id=(d, s + 1), device_id_type=MESH)
-
-    def to_below():
-        return pltpu.make_async_remote_copy(
-            rot.at[0], rot_in.at[1], rot_s.at[1], rot_r.at[1], device_id=(d, s - 1), device_id_type=MESH)
-
-    @pl.when(s < 3)
-    def _():
-        to_above().start()
-
-    @pl.when(s > 0)
-    def _():
-        to_below().start()
-
-    zero_blk[...] = jnp.zeros_like(zero_blk)
     half[16] = jnp.zeros((256, 256), BF16)
 
     def flip(i, _):
@@ -84,6 +63,9 @@
         return 0
 
     lax.fori_loop(0, 4, flip, 0)
+    rot_t[0] = jnp.zeros((256, 256), BF16)
+    rot_t[5] = jnp.zeros((256, 256), BF16)
+    reg[1] = jnp.zeros((4, 256, 256), BF16)
 
     loads[1].wait()
     for p in range(4):
@@ -98,7 +80,7 @@
 
         lax.fori_loop(0, 4, stage_one, 0)
 
-    kinds = [dirs[p, 0] for p in range(4)]
+    kinds = [dirs[p] for p in range(4)]
     fresh = []
     for p in range(4):
         seen = jnp.int32(0)
@@ -113,60 +95,64 @@
         first[k] = pick
     extra = 6 - first[1] - first[2] - first[3]
     extra = jnp.clip(extra, 0, 3)
-    extra_kind = dirs[extra, 0]
-
-    @pl.when(s > 0)
-    def _():
-        to_above().wait_recv()
-        rot_t[0] = rot_in[0].T
-
-    @pl.when(s == 0)
-    def _():
-        rot_t[0] = jnp.zeros((256, 256), BF16)
-
-    @pl.when(s < 3)
-    def _():
-        to_below().wait_recv()
-        rot_t[5] = rot_in[1].T
-
-    @pl.when(s == 3)
-    def _():
-        rot_t[5] = jnp.zeros((256, 256), BF16)
-
-    def moved(k, j):
+    extra_kind = dirs[extra]
+
+    sides = jnp.where(s > 0, 2, 0) + jnp.where(s < 3, 2, 0)
+    pl.semaphore_wait(bar, 10 + sides)
+
+    def to_above():
+        return pltpu.make_async_remote_copy(
+            rot.at[3], rot_in.at[0], rot_s.at[0], rot_r.at[0], device_id=(d, s + 1), device_id_type=MESH)
+
+    def to_below():
+        return pltpu.make_async_remote_copy(
+            rot.at[0], rot_in.at[1], rot_s.at[1], rot_r.at[1], device_id=(d, s - 1), device_id_type=MESH)
+
+    @pl.when(s < 3)
+    def _():
+        to_above().start()
+
+    @pl.when(s > 0)
+    def _():
+        to_below().start()
+
+
+    def moved(k, j, part_no):
         to = {1: up, 2: down, 3: across}[k]
         n = 2 * (k - 1) + j
+        cut = (pl.ds(0, 1), pl.ds(1, 2), pl.ds(3, 1))[part_no]
         return pltpu.make_async_remote_copy(
-            pay.at[n], reg.at[2 * k + j], pay_s.at[n], pay_r.at[n], device_id=(to, s), device_id_type=MESH)
+            pay.at[n, cut], reg.at[2 * k + j, cut], pay_s.at[n, part_no], pay_r.at[n, part_no],
+            device_id=(to, s), device_id_type=MESH)
 
     def renormed(p, i):
         w = pres[p, i].astype(F32)
         return jnp.dot(rot_t[i + 1 + chg[p]], rotd[4 * p + i], preferred_element_type=F32) * w
 
-    for k in (3, 1, 2):
-        pair = first[k]
-
-        def stage_two(i, _, pair=pair, k=k):
-            pay[2 * (k - 1), i] = renormed(pair, i).astype(BF16)
+    def firsts(k, i):
+        pay[2 * (k - 1), i] = renormed(first[k], i).astype(BF16)
+
+    def extras(i):
+        block = renormed(extra, i)
+        for k in (1, 2, 3):
+            pay[2 * (k - 1) + 1, i] = (block * (extra_kind == k).astype(F32)).astype(BF16)
+        reg[0, i] = (block * (extra_kind == 0).astype(F32)).astype(BF16)
+
+    for k in (1, 2, 3):
+        def inner(i, _, k=k):
+            firsts(k, i)
             return 0
 
-        lax.fori_loop(0, 4, stage_two, 0)
-        moved(k, 0).start()
-
-    def stage_three(i, _):
-        block = renormed(extra, i)
-        for k in (3, 1, 2):
-            pay[2 * (k - 1) + 1, i] = (block * (extra_kind == k).astype(F32)).astype(BF16)
-        pay[6, i] = (block * (extra_kind == 0).astype(F32)).astype(BF16)
-        return 0
-
-    lax.fori_loop(0, 4, stage_three, 0)
-    for k in (3, 1, 2):
-        moved(k, 1).start()
-    stay = pltpu.make_async_copy(pay.at[6], reg.at[0], loc_sem.at[0])
-    blank = pltpu.make_async_copy(zero_blk, reg.at[1], loc_sem.at[1])
-    stay.start()
-    blank.start()
+        lax.fori_loop(1, 3, inner, 0)
+        moved(k, 0, 1).start()
+
+    def inner_extra(i, _):
+        extras(i)
+        return 0
+
+    lax.fori_loop(1, 3, inner_extra, 0)
+    for k in (1, 2, 3):
+        moved(k, 1, 1).start()
 
     loads[6].wait()
     row = lax.broadcasted_iota(jnp.int32, (256, 256), 0)
@@ -192,7 +178,33 @@
     to_core = pltpu.make_async_remote_copy(
         part.at[:, 1 - c], c_in, c_s.at[0], c_r.at[0], device_id=(core_peer, s), device_id_type=MESH)
     to_core.start()
-    to_core.wait()
+
+    @pl.when(s > 0)
+    def _():
+        to_above().wait_recv()
+        rot_t[0] = rot_in[0].T
+
+    @pl.when(s < 3)
+    def _():
+        to_below().wait_recv()
+        rot_t[5] = rot_in[1].T
+
+    def outer(q, _):
+        for k in (1, 2, 3):
+            firsts(k, 3 * q)
+        extras(3 * q)
+        return 0
+
+    lax.fori_loop(0, 2, outer, 0)
+
+    def send_outer(k):
+        for j in (0, 1):
+            for part_no in (0, 2):
+                moved(k, j, part_no).start()
+
+    far_up = jnp.logical_and(x == 3, c == 1)
+    far_down = jnp.logical_and(x == 0, c == 0)
+    to_core.wait_recv()
 
     def core_sum(e, _):
         both = part[e, c].astype(F32) + c_in[e].astype(F32)
@@ -207,8 +219,17 @@
             device_id=(x_peer[o], s), device_id_type=MESH)
         copy.start()
         to_x.append(copy)
+
+    @pl.when(jnp.logical_not(far_up))
+    def _():
+        send_outer(1)
+
+    @pl.when(jnp.logical_not(far_down))
+    def _():
+        send_outer(2)
+
     for copy in to_x:
-        copy.wait()
+        copy.wait_recv()
     rows = pl.ds(pl.multiple_of(x * 32, 32), 32)
 
     def x_sum(e, _):
@@ -229,8 +250,9 @@
             device_id=(y_peer[o], s), device_id_type=MESH)
         copy.start()
         to_y.append(copy)
+    send_outer(3)
     for copy in to_y:
-        copy.wait()
+        copy.wait_recv()
     total = f2[y].reshape(48, 256)
     for o in range(3):
         total = total + y_in[o].astype(F32)
@@ -258,7 +280,15 @@
         edge(0, 0).start()
         edge(0, 1).start()
 
-    to_z.wait()
+    @pl.when(far_up)
+    def _():
+        send_outer(1)
+
+    @pl.when(far_down)
+    def _():
+        send_outer(2)
+
+    to_z.wait_recv()
     mine = (total[8:40] + z_in[...].astype(F32)).reshape(4, 8, 256)
     f2[0, pl.ds(0, 4)] = mine
 
@@ -277,6 +307,9 @@
     final = f2[0, pl.ds(0, 4)] * (1.0 / 16.0)
     sig[...] = jnp.where(zh == 0, final[:, 0:4], final[:, 4:8])
 
+    for copy in [to_core, to_z] + to_x + to_y:
+        copy.wait_send()
+
     @pl.when(s < 3)
     def _():
         edge(1, 0).wait_send()
@@ -289,25 +322,25 @@
         edge(0, 1).wait_send()
         to_below().wait_send()
 
-    for k in (3, 1, 2):
+    for k in (1, 2, 3):
         for j in (0, 1):
-            moved(k, j).wait()
-    stay.wait()
-    blank.wait()
+            for part_no in range(3):
+                moved(k, j, part_no).wait()
 
 
 def body(wavefunction, left_operators, right_operators, rotations, charges, present_blocks, directions):
     hbm = pl.BlockSpec(memory_space=pltpu.HBM)
+    vmem = pl.BlockSpec(memory_space=pltpu.VMEM)
     smem = pl.BlockSpec(memory_space=pltpu.SMEM)
     dma = pltpu.SemaphoreType.DMA
     sigma, regrouped = pl.pallas_call(
         kernel,
         out_shape=(
-            jax.ShapeDtypeStruct((4, 4, 256), F32),
-            jax.ShapeDtypeStruct((8, 4, 256, 256), BF16),
+            pltpu.VMEM((4, 4, 256), F32),
+            pltpu.VMEM((8, 4, 256, 256), BF16),
         ),
         in_specs=[smem, smem, smem, hbm, hbm, hbm, hbm],
-        out_specs=(pl.BlockSpec(memory_space=pltpu.VMEM), hbm),
+        out_specs=(vmem, vmem),
         scratch_shapes=[
             pltpu.VMEM((4, 256, 256), BF16),
             pltpu.VMEM((16, 256, 256), BF16),
@@ -317,8 +350,7 @@
             pltpu.VMEM((2, 256, 256), BF16),
             pltpu.VMEM((17, 256, 256), BF16),
             pltpu.VMEM((16, 256, 256), BF16),
-            pltpu.VMEM((7, 4, 256, 256), BF16),
-            pltpu.VMEM((4, 256, 256), BF16),
+            pltpu.VMEM((6, 4, 256, 256), BF16),
             pltpu.VMEM((6, 2, 128, 256), BF16),
             pltpu.VMEM((6, 128, 256), BF16),
             pltpu.VMEM((6, 4, 32, 256), BF16),
@@ -330,15 +362,15 @@
             pltpu.VMEM((32, 256), BF16),
             pltpu.VMEM((2, 8, 256), F32),
             pltpu.VMEM((2, 2, 8, 256), F32),
-            dma((7,)), dma((2,)), dma((2,)), dma((6,)), dma((6,)), dma((2,)),
+            dma((7,)), dma((2,)), dma((2,)), dma((6, 3)), dma((6, 3)),
             dma((1,)), dma((1,)), dma((3,)), dma((3,)), dma((3,)), dma((3,)),
             dma((1,)), dma((1,)), dma((2, 2)), dma((2, 2)),
         ],
         compiler_params=pltpu.CompilerParams(
-            collective_id=0, has_side_effects=True, vmem_limit_bytes=48 * 1024 * 1024),
+            collective_id=0, has_side_effects=True, vmem_limit_bytes=58000000),
         name="step",
     )(
-        charges, present_blocks, directions,
+        charges, present_blocks, directions.reshape(4),
         wavefunction,
         left_operators.reshape(16, 256, 256),
         right_operators.reshape(16, 256, 256),

time: 72.3 us -> 61.8 us (0.85)
  the two profiles are of different devices: /device:TPU:6 before, /device:TPU:16 now
where the time goes in v2:
time: 61.8 us; the launch traced here: 61.7 us
  Pallas kernels  58.4 us (94%)
  local copies, waits for them, and re-layouts  2.62 us (4%)
  between operations  0.64 us (1%)
    pallas_call x1, Pallas kernels, body(): pl.pallas_call(kernel, out_shape=(pltpu.VMEM((4, 4, 256), F32), pltpu.VME...  58.4 us
    unnamed x2, local copies, waits for them, and re-layouts  2.62 us

profile of v2, /device:TPU:16, one launch (start us, length us, event | category | flops | bytes accessed | tf_op | source)
XLA Modules:
  0.0 61.7 jit_solution(14966803852086995672)
XLA Ops:
  0.6 58.4 %step.1 = (f32[4,4,256]{2,1,0:T(4,128)S(1)}, bf16[8,4,256,256]{3,2,1,0:T(8,128)(2,1)S(1)}) custom-call(s32[4]{0:T(128)} %chg.1, s32[4,4]{1,0:T(4,128)} %pres.1, s32[4]{0:T(128)} %bitcast.5, bf16[4,256,256]{2,1,0:T(8,128)(2,1)} %psi_h.1, bf16[16,256,256]{2,1,0:T(8,128)(2,1)} %bitcast.3, bf16[16,256,256]{2,1,0:T(8,128)(2,1)} %bitcast.4, bf16[4,256,256]{2,1,0:T(8,128)(2,1)} %rot_h.1), custom_call_target="tpu_custom_call" | custom-call | tf_op jit(solution)/shard_map/step/pallas_call | solution.py:336
  59.0 0.6 copy.11
  59.7 2.0 %copy.12 = bf16[8,4,256,256]{3,2,1,0:T(8,128)(2,1)} copy(bf16[8,4,256,256]{3,2,1,0:T(8,128)(2,1)S(1)} %get-tuple-element.3) | data formatting | bytes 8388608

commit v3 on v2

--- a/solution.py
+++ b/solution.py
@@ -18,9 +18,9 @@
 def kernel(
     chg, pres, dirs, psi_h, left_h, right_h, rot_h,
     sig, reg,
-    psi, left, right, rot, rot_t, rot_in, half, rotd, pay,
+    psi, left, right, rot, rot_t, rot_in, half, rotd, pay, hand,
     part, c_in, x_out, x_in, f2, y_out, y_in, z_out, z_in, e_out, e_in,
-    in_sem, rot_s, rot_r, pay_s, pay_r, c_s, c_r, x_s, x_r, y_s, y_r, z_s, z_r, e_s, e_r,
+    in_sem, rot_s, rot_r, pay_s, pay_r, hand_s, hand_r, c_s, c_r, x_s, x_r, y_s, y_r, z_s, z_r, e_s, e_r,
 ):
     d = lax.axis_index("op")
     s = lax.axis_index("sec")
@@ -31,12 +31,23 @@
     zh_peer = place(y, 1 - zh, x, c)
     up, down, across = (d + 1) % 64, (d + 63) % 64, (d + 32) % 64
 
-    loads = [
-        pltpu.make_async_copy(rot_h, rot, in_sem.at[0]),
-        pltpu.make_async_copy(psi_h, psi, in_sem.at[1]),
-    ]
+    far_up = jnp.logical_and(x == 3, c == 1)
+    far_down = jnp.logical_and(x == 0, c == 0)
+    hand_up = jnp.logical_and(x == 2, c == 0)
+    hand_down = jnp.logical_and(x == 1, c == 1)
+    via_up = place((y + zh) % 4, zh, 2, 0)
+    via_down = place((y + 3 + zh) % 4, zh, 1, 1)
+    late_up = place(y, 1 - zh, 2, 0)
+    late_down = place(y, 1 - zh, 1, 1)
+    from_up = place((y + 4 - zh) % 4, zh, 3, 1)
+    from_down = place((y + 1 - zh) % 4, zh, 0, 0)
+    onto_up = place(y, 1 - zh, 0, 0)
+    onto_down = place(y, 1 - zh, 3, 1)
+
+    loads = [pltpu.make_async_copy(rot_h, rot, in_sem.at[0])]
     for p in range(4):
-        loads.append(pltpu.make_async_copy(left_h.at[pl.ds(4 * p, 4)], left.at[pl.ds(4 * p, 4)], in_sem.at[2 + p]))
+        loads.append(pltpu.make_async_copy(left_h.at[pl.ds(4 * p, 4)], left.at[pl.ds(4 * p, 4)], in_sem.at[1 + p]))
+    loads.append(pltpu.make_async_copy(psi_h, psi, in_sem.at[5]))
     loads.append(pltpu.make_async_copy(right_h, right, in_sem.at[6]))
 
     bar = pltpu.get_barrier_semaphore()
@@ -52,6 +63,17 @@
     def _():
         for peer in (d, zh_peer):
             pl.semaphore_signal(bar, inc=1, device_id=(peer, s + 1), device_id_type=MESH)
+
+    def greet(when, peers):
+        @pl.when(when)
+        def _():
+            for peer in peers:
+                pl.semaphore_signal(bar, inc=1, device_id=(peer, s), device_id_type=MESH)
+
+    greet(far_up, (via_up, late_down))
+    greet(far_down, (via_down, late_up))
+    greet(hand_up, (from_up, onto_up))
+    greet(hand_down, (from_down, onto_down))
 
     for copy in loads:
         copy.start()
@@ -67,18 +89,18 @@
     rot_t[5] = jnp.zeros((256, 256), BF16)
     reg[1] = jnp.zeros((4, 256, 256), BF16)
 
-    loads[1].wait()
     for p in range(4):
-        loads[2 + p].wait()
-
-        def stage_one(i, _, p=p):
-            block = left[4 * p + i]
-            w = pres[p, i].astype(F32)
-            half[4 * p + i] = (jnp.dot(block, psi[i], preferred_element_type=F32) * w).astype(BF16)
-            rotd[4 * p + i] = jnp.dot(block, rot[i], preferred_element_type=F32).astype(BF16)
-            return 0
-
-        lax.fori_loop(0, 4, stage_one, 0)
+        loads[1 + p].wait()
+
+    def rotate(p, i):
+        rotd[4 * p + i] = jnp.dot(left[4 * p + i], rot[i], preferred_element_type=F32).astype(BF16)
+
+    def rotate_inner(p, _):
+        rotate(p, 1)
+        rotate(p, 2)
+        return 0
+
+    lax.fori_loop(0, 4, rotate_inner, 0)
 
     kinds = [dirs[p] for p in range(4)]
     fresh = []
@@ -97,9 +119,6 @@
     extra = jnp.clip(extra, 0, 3)
     extra_kind = dirs[extra]
 
-    sides = jnp.where(s > 0, 2, 0) + jnp.where(s < 3, 2, 0)
-    pl.semaphore_wait(bar, 10 + sides)
-
     def to_above():
         return pltpu.make_async_remote_copy(
             rot.at[3], rot_in.at[0], rot_s.at[0], rot_r.at[0], device_id=(d, s + 1), device_id_type=MESH)
@@ -108,22 +127,62 @@
         return pltpu.make_async_remote_copy(
             rot.at[0], rot_in.at[1], rot_s.at[1], rot_r.at[1], device_id=(d, s - 1), device_id_type=MESH)
 
-    @pl.when(s < 3)
-    def _():
-        to_above().start()
-
-    @pl.when(s > 0)
-    def _():
-        to_below().start()
-
-
-    def moved(k, j, part_no):
+    def moved(k, j, i):
         to = {1: up, 2: down, 3: across}[k]
         n = 2 * (k - 1) + j
-        cut = (pl.ds(0, 1), pl.ds(1, 2), pl.ds(3, 1))[part_no]
-        return pltpu.make_async_remote_copy(
-            pay.at[n, cut], reg.at[2 * k + j, cut], pay_s.at[n, part_no], pay_r.at[n, part_no],
+        return pltpu.make_async_remote_copy(
+            pay.at[n, i], reg.at[2 * k + j, i], pay_s.at[n, i], pay_r.at[n, i],
             device_id=(to, s), device_id_type=MESH)
+
+    def to_hand(k, j, i):
+        n, h = 2 * (k - 1) + j, 2 * (i - 1) + j
+        return pltpu.make_async_remote_copy(
+            pay.at[n, i], hand.at[h], pay_s.at[n, i], hand_r.at[h],
+            device_id=({1: via_up, 2: via_down}[k], s), device_id_type=MESH)
+
+    def from_hand(k, j, i):
+        n, h = 2 * (k - 1) + j, 2 * (i - 1) + j
+        return pltpu.make_async_remote_copy(
+            hand.at[h], reg.at[2 * k + j, i], hand_s.at[h], pay_r.at[n, i],
+            device_id=({1: onto_up, 2: onto_down}[k], s), device_id_type=MESH)
+
+    def send_far(sectors):
+        for k, far in ((1, far_up), (2, far_down)):
+            @pl.when(far)
+            def _(k=k):
+                for i in sectors:
+                    for j in (0, 1):
+                        (to_hand if i in (1, 2) else moved)(k, j, i).start()
+
+    def send_beside(sectors):
+        for k, here in ((1, c == 0), (2, c == 1)):
+            @pl.when(here)
+            def _(k=k):
+                for i in sectors:
+                    for j in (0, 1):
+                        moved(k, j, i).start()
+
+    def send_ring(sectors):
+        for k, here in ((1, (c == 1) & (x < 3)), (2, (c == 0) & (x > 0))):
+            @pl.when(here)
+            def _(k=k):
+                for i in sectors:
+                    for j in (0, 1):
+                        moved(k, j, i).start()
+
+    def send_across(sectors):
+        for i in sectors:
+            for j in (0, 1):
+                moved(3, j, i).start()
+
+    def hand_on():
+        for k, here in ((1, hand_up), (2, hand_down)):
+            @pl.when(here)
+            def _(k=k):
+                for i in (1, 2):
+                    for j in (0, 1):
+                        to_hand(k, j, i).wait_recv()
+                        from_hand(k, j, i).start()
 
     def renormed(p, i):
         w = pres[p, i].astype(F32)
@@ -138,22 +197,66 @@
             pay[2 * (k - 1) + 1, i] = (block * (extra_kind == k).astype(F32)).astype(BF16)
         reg[0, i] = (block * (extra_kind == 0).astype(F32)).astype(BF16)
 
-    for k in (1, 2, 3):
-        def inner(i, _, k=k):
+    def all_of(i):
+        for k in (1, 2, 3):
             firsts(k, i)
-            return 0
-
-        lax.fori_loop(1, 3, inner, 0)
-        moved(k, 0, 1).start()
-
-    def inner_extra(i, _):
         extras(i)
-        return 0
-
-    lax.fori_loop(1, 3, inner_extra, 0)
-    for k in (1, 2, 3):
-        moved(k, 1, 1).start()
-
+
+    def inner(i, _):
+        all_of(i)
+        return 0
+
+    lax.fori_loop(1, 3, inner, 0)
+    sides = jnp.where(s > 0, 2, 0) + jnp.where(s < 3, 2, 0)
+    corner = far_up | far_down | hand_up | hand_down
+    pl.semaphore_wait(bar, 10 + sides + jnp.where(corner, 2, 0))
+
+    @pl.when(s < 3)
+    def _():
+        to_above().start()
+
+    @pl.when(s > 0)
+    def _():
+        to_below().start()
+
+    send_far((1, 2))
+    send_across((1, 2))
+    send_beside((1, 2))
+
+    loads[5].wait()
+
+    def halve(p, _):
+        for i in range(4):
+            w = pres[p, i].astype(F32)
+            half[4 * p + i] = (jnp.dot(left[4 * p + i], psi[i], preferred_element_type=F32) * w).astype(BF16)
+        return 0
+
+    lax.fori_loop(0, 4, halve, 0)
+
+    def rotate_outer(p, _):
+        rotate(p, 0)
+        rotate(p, 3)
+        return 0
+
+    lax.fori_loop(0, 4, rotate_outer, 0)
+
+    @pl.when(s > 0)
+    def _():
+        to_above().wait_recv()
+        rot_t[0] = rot_in[0].T
+
+    @pl.when(s < 3)
+    def _():
+        to_below().wait_recv()
+        rot_t[5] = rot_in[1].T
+
+    def outer(q, _):
+        all_of(3 * q)
+        return 0
+
+    lax.fori_loop(0, 2, outer, 0)
+    send_far((0, 3))
+    send_across((0, 3))
     loads[6].wait()
     row = lax.broadcasted_iota(jnp.int32, (256, 256), 0)
     col = lax.broadcasted_iota(jnp.int32, (256, 256), 1)
@@ -173,63 +276,37 @@
         part[e, 1] = placed[128:]
         return 0
 
-    lax.fori_loop(0, 6, target_sum, 0)
-
-    to_core = pltpu.make_async_remote_copy(
-        part.at[:, 1 - c], c_in, c_s.at[0], c_r.at[0], device_id=(core_peer, s), device_id_type=MESH)
-    to_core.start()
-
-    @pl.when(s > 0)
-    def _():
-        to_above().wait_recv()
-        rot_t[0] = rot_in[0].T
-
-    @pl.when(s < 3)
-    def _():
-        to_below().wait_recv()
-        rot_t[5] = rot_in[1].T
-
-    def outer(q, _):
-        for k in (1, 2, 3):
-            firsts(k, 3 * q)
-        extras(3 * q)
-        return 0
-
-    lax.fori_loop(0, 2, outer, 0)
-
-    def send_outer(k):
-        for j in (0, 1):
-            for part_no in (0, 2):
-                moved(k, j, part_no).start()
-
-    far_up = jnp.logical_and(x == 3, c == 1)
-    far_down = jnp.logical_and(x == 0, c == 0)
-    to_core.wait_recv()
+    def to_core(g):
+        some = pl.ds(3 * g, 3)
+        return pltpu.make_async_remote_copy(
+            part.at[some, 1 - c], c_in.at[some], c_s.at[g], c_r.at[g], device_id=(core_peer, s), device_id_type=MESH)
+
+    def to_x(g, o):
+        some = pl.ds(3 * g, 3)
+        return pltpu.make_async_remote_copy(
+            x_out.at[some, (x + o + 1) % 4], x_in.at[o, some], x_s.at[g, o], x_r.at[g, o],
+            device_id=(x_peer[o], s), device_id_type=MESH)
+
+    for g in (0, 1):
+        lax.fori_loop(3 * g, 3 * g + 3, target_sum, 0)
+        to_core(g).start()
 
     def core_sum(e, _):
         both = part[e, c].astype(F32) + c_in[e].astype(F32)
         x_out[e] = both.reshape(4, 32, 256).astype(BF16)
         return 0
 
-    lax.fori_loop(0, 6, core_sum, 0)
-    to_x = []
-    for o in range(3):
-        copy = pltpu.make_async_remote_copy(
-            x_out.at[:, (x + o + 1) % 4], x_in.at[o], x_s.at[o], x_r.at[o],
-            device_id=(x_peer[o], s), device_id_type=MESH)
-        copy.start()
-        to_x.append(copy)
-
-    @pl.when(jnp.logical_not(far_up))
-    def _():
-        send_outer(1)
-
-    @pl.when(jnp.logical_not(far_down))
-    def _():
-        send_outer(2)
-
-    for copy in to_x:
-        copy.wait_recv()
+    for g in (0, 1):
+        to_core(g).wait_recv()
+        lax.fori_loop(3 * g, 3 * g + 3, core_sum, 0)
+        for o in range(3):
+            to_x(g, o).start()
+    hand_on()
+    send_beside((0, 3))
+    send_ring((0, 1, 2, 3))
+    for g in (0, 1):
+        for o in range(3):
+            to_x(g, o).wait_recv()
     rows = pl.ds(pl.multiple_of(x * 32, 32), 32)
 
     def x_sum(e, _):
@@ -250,7 +327,6 @@
             device_id=(y_peer[o], s), device_id_type=MESH)
         copy.start()
         to_y.append(copy)
-    send_outer(3)
     for copy in to_y:
         copy.wait_recv()
     total = f2[y].reshape(48, 256)
@@ -280,14 +356,6 @@
         edge(0, 0).start()
         edge(0, 1).start()
 
-    @pl.when(far_up)
-    def _():
-        send_outer(1)
-
-    @pl.when(far_down)
-    def _():
-        send_outer(2)
-
     to_z.wait_recv()
     mine = (total[8:40] + z_in[...].astype(F32)).reshape(4, 8, 256)
     f2[0, pl.ds(0, 4)] = mine
@@ -307,8 +375,12 @@
     final = f2[0, pl.ds(0, 4)] * (1.0 / 16.0)
     sig[...] = jnp.where(zh == 0, final[:, 0:4], final[:, 4:8])
 
-    for copy in [to_core, to_z] + to_x + to_y:
+    for copy in [to_z] + to_y:
         copy.wait_send()
+    for g in (0, 1):
+        to_core(g).wait_send()
+        for o in range(3):
+            to_x(g, o).wait_send()
 
     @pl.when(s < 3)
     def _():
@@ -322,10 +394,17 @@
         edge(0, 1).wait_send()
         to_below().wait_send()
 
+    for k, here in ((1, hand_up), (2, hand_down)):
+        @pl.when(here)
+        def _(k=k):
+            for j in (0, 1):
+                for i in (1, 2):
+                    from_hand(k, j, i).wait_send()
+
     for k in (1, 2, 3):
         for j in (0, 1):
-            for part_no in range(3):
-                moved(k, j, part_no).wait()
+            for i in range(4):
+                moved(k, j, i).wait()
 
 
 def body(wavefunction, left_operators, right_operators, rotations, charges, present_blocks, directions):
@@ -351,6 +430,7 @@
             pltpu.VMEM((17, 256, 256), BF16),
             pltpu.VMEM((16, 256, 256), BF16),
             pltpu.VMEM((6, 4, 256, 256), BF16),
+            pltpu.VMEM((4, 256, 256), BF16),
             pltpu.VMEM((6, 2, 128, 256), BF16),
             pltpu.VMEM((6, 128, 256), BF16),
             pltpu.VMEM((6, 4, 32, 256), BF16),
@@ -362,8 +442,8 @@
             pltpu.VMEM((32, 256), BF16),
             pltpu.VMEM((2, 8, 256), F32),
             pltpu.VMEM((2, 2, 8, 256), F32),
-            dma((7,)), dma((2,)), dma((2,)), dma((6, 3)), dma((6, 3)),
-            dma((1,)), dma((1,)), dma((3,)), dma((3,)), dma((3,)), dma((3,)),
+            dma((7,)), dma((2,)), dma((2,)), dma((6, 4)), dma((6, 4)), dma((4,)), dma((4,)),
+            dma((2,)), dma((2,)), dma((2, 3)), dma((2, 3)), dma((3,)), dma((3,)),
             dma((1,)), dma((1,)), dma((2, 2)), dma((2, 2)),
         ],
         compiler_params=pltpu.CompilerParams(

time: 61.8 us -> 51.3 us (0.83)
  the two profiles are of different devices: /device:TPU:16 before, /device:TPU:6 now
where the time goes in v3:
time: 51.3 us; the launch traced here: 51.2 us
  Pallas kernels  47.9 us (93%)
  local copies, waits for them, and re-layouts  2.62 us (5%)
  between operations  0.64 us (1%)
    pallas_call x1, Pallas kernels, body(): pl.pallas_call(kernel, out_shape=(pltpu.VMEM((4, 4, 256), F32), pltpu.VME...  47.9 us
    unnamed x2, local copies, waits for them, and re-layouts  2.62 us

profile of v3, /device:TPU:6, one launch (start us, length us, event | category | flops | bytes accessed | tf_op | source)
XLA Modules:
  0.0 51.2 jit_solution(1839502549479542680)
XLA Ops:
  0.6 47.9 %step.1 = (f32[4,4,256]{2,1,0:T(4,128)S(1)}, bf16[8,4,256,256]{3,2,1,0:T(8,128)(2,1)S(1)}) custom-call(s32[4]{0:T(128)} %chg.1, s32[4,4]{1,0:T(4,128)} %pres.1, s32[4]{0:T(128)} %bitcast.5, bf16[4,256,256]{2,1,0:T(8,128)(2,1)} %psi_h.1, bf16[16,256,256]{2,1,0:T(8,128)(2,1)} %bitcast.3, bf16[16,256,256]{2,1,0:T(8,128)(2,1)} %bitcast.4, bf16[4,256,256]{2,1,0:T(8,128)(2,1)} %rot_h.1), custom_call_target="tpu_custom_call" | custom-call | tf_op jit(solution)/shard_map/step/pallas_call | solution.py:415
  48.5 0.6 %copy.11 = f32[4,4,256]{2,1,0:T(4,128)} copy(f32[4,4,256]{2,1,0:T(4,128)S(1)} %get-tuple-element.2) | data formatting | bytes 32768
  49.1 2.0 %copy.12 = bf16[8,4,256,256]{3,2,1,0:T(8,128)(2,1)} copy(bf16[8,4,256,256]{3,2,1,0:T(8,128)(2,1)S(1)} %get-tuple-element.3) | data formatting | bytes 8388608

commit v4 on v3

--- a/solution.py
+++ b/solution.py
@@ -46,7 +46,8 @@
 
     loads = [pltpu.make_async_copy(rot_h, rot, in_sem.at[0])]
     for p in range(4):
-        loads.append(pltpu.make_async_copy(left_h.at[pl.ds(4 * p, 4)], left.at[pl.ds(4 * p, 4)], in_sem.at[1 + p]))
+        i = (1, 2, 0, 3)[p]
+        loads.append(pltpu.make_async_copy(left_h.at[:, i], left.at[i], in_sem.at[1 + p]))
     loads.append(pltpu.make_async_copy(psi_h, psi, in_sem.at[5]))
     loads.append(pltpu.make_async_copy(right_h, right, in_sem.at[6]))
 
@@ -89,18 +90,13 @@
     rot_t[5] = jnp.zeros((256, 256), BF16)
     reg[1] = jnp.zeros((4, 256, 256), BF16)
 
-    for p in range(4):
-        loads[1 + p].wait()
-
-    def rotate(p, i):
-        rotd[4 * p + i] = jnp.dot(left[4 * p + i], rot[i], preferred_element_type=F32).astype(BF16)
-
-    def rotate_inner(p, _):
-        rotate(p, 1)
-        rotate(p, 2)
-        return 0
-
-    lax.fori_loop(0, 4, rotate_inner, 0)
+    def rotate(i):
+        rows = left[i].reshape(1024, 256)
+        rotd[pl.ds(4 * i, 4)] = jnp.dot(rows, rot[i], preferred_element_type=F32).astype(BF16).reshape(4, 256, 256)
+
+    for i in (1, 2):
+        loads[i].wait()
+        rotate(i)
 
     kinds = [dirs[p] for p in range(4)]
     fresh = []
@@ -135,13 +131,13 @@
             device_id=(to, s), device_id_type=MESH)
 
     def to_hand(k, j, i):
-        n, h = 2 * (k - 1) + j, 2 * (i - 1) + j
+        n, h = 2 * (k - 1) + j, 2 * i + j
         return pltpu.make_async_remote_copy(
             pay.at[n, i], hand.at[h], pay_s.at[n, i], hand_r.at[h],
             device_id=({1: via_up, 2: via_down}[k], s), device_id_type=MESH)
 
     def from_hand(k, j, i):
-        n, h = 2 * (k - 1) + j, 2 * (i - 1) + j
+        n, h = 2 * (k - 1) + j, 2 * i + j
         return pltpu.make_async_remote_copy(
             hand.at[h], reg.at[2 * k + j, i], hand_s.at[h], pay_r.at[n, i],
             device_id=({1: onto_up, 2: onto_down}[k], s), device_id_type=MESH)
@@ -152,7 +148,7 @@
             def _(k=k):
                 for i in sectors:
                     for j in (0, 1):
-                        (to_hand if i in (1, 2) else moved)(k, j, i).start()
+                        (to_hand if i in (0, 1, 2) else moved)(k, j, i).start()
 
     def send_beside(sectors):
         for k, here in ((1, c == 0), (2, c == 1)):
@@ -175,18 +171,18 @@
             for j in (0, 1):
                 moved(3, j, i).start()
 
-    def hand_on():
+    def hand_on(sectors):
         for k, here in ((1, hand_up), (2, hand_down)):
             @pl.when(here)
             def _(k=k):
-                for i in (1, 2):
+                for i in sectors:
                     for j in (0, 1):
                         to_hand(k, j, i).wait_recv()
                         from_hand(k, j, i).start()
 
     def renormed(p, i):
         w = pres[p, i].astype(F32)
-        return jnp.dot(rot_t[i + 1 + chg[p]], rotd[4 * p + i], preferred_element_type=F32) * w
+        return jnp.dot(rot_t[i + 1 + chg[p]], rotd[4 * i + p], preferred_element_type=F32) * w
 
     def firsts(k, i):
         pay[2 * (k - 1), i] = renormed(first[k], i).astype(BF16)
@@ -223,40 +219,18 @@
     send_across((1, 2))
     send_beside((1, 2))
 
+    loads[3].wait()
+    loads[4].wait()
     loads[5].wait()
 
-    def halve(p, _):
-        for i in range(4):
-            w = pres[p, i].astype(F32)
-            half[4 * p + i] = (jnp.dot(left[4 * p + i], psi[i], preferred_element_type=F32) * w).astype(BF16)
+    def halve(i, _):
+        both = jnp.dot(left[i].reshape(1024, 256), psi[i], preferred_element_type=F32).reshape(4, 256, 256)
+        for p in range(4):
+            half[4 * i + p] = (both[p] * pres[p, i].astype(F32)).astype(BF16)
         return 0
 
     lax.fori_loop(0, 4, halve, 0)
 
-    def rotate_outer(p, _):
-        rotate(p, 0)
-        rotate(p, 3)
-        return 0
-
-    lax.fori_loop(0, 4, rotate_outer, 0)
-
-    @pl.when(s > 0)
-    def _():
-        to_above().wait_recv()
-        rot_t[0] = rot_in[0].T
-
-    @pl.when(s < 3)
-    def _():
-        to_below().wait_recv()
-        rot_t[5] = rot_in[1].T
-
-    def outer(q, _):
-        all_of(3 * q)
-        return 0
-
-    lax.fori_loop(0, 2, outer, 0)
-    send_far((0, 3))
-    send_across((0, 3))
     loads[6].wait()
     row = lax.broadcasted_iota(jnp.int32, (256, 256), 0)
     col = lax.broadcasted_iota(jnp.int32, (256, 256), 1)
@@ -269,7 +243,7 @@
             src = e - 1 - chg[p]
             inside = jnp.logical_and(src >= 0, src <= 3)
             clipped = jnp.clip(src, 0, 3)
-            lhs = half[jnp.where(inside, 4 * p + clipped, 16)]
+            lhs = half[jnp.where(inside, 4 * clipped + p, 16)]
             total = total + lax.dot_general(lhs, right[4 * p + clipped], NT, preferred_element_type=F32)
         placed = jnp.dot(order, total.astype(BF16), preferred_element_type=F32).astype(BF16)
         part[e, 0] = placed[:128]
@@ -291,6 +265,26 @@
         lax.fori_loop(3 * g, 3 * g + 3, target_sum, 0)
         to_core(g).start()
 
+    for i in (0, 3):
+        rotate(i)
+
+    @pl.when(s > 0)
+    def _():
+        to_above().wait_recv()
+        rot_t[0] = rot_in[0].T
+
+    @pl.when(s < 3)
+    def _():
+        to_below().wait_recv()
+        rot_t[5] = rot_in[1].T
+
+    def outer(q, _):
+        all_of(3 * q)
+        return 0
+
+    lax.fori_loop(0, 2, outer, 0)
+    send_far((0, 3))
+    send_across((0,))
     def core_sum(e, _):
         both = part[e, c].astype(F32) + c_in[e].astype(F32)
         x_out[e] = both.reshape(4, 32, 256).astype(BF16)
@@ -301,7 +295,7 @@
         lax.fori_loop(3 * g, 3 * g + 3, core_sum, 0)
         for o in range(3):
             to_x(g, o).start()
-    hand_on()
+    hand_on((1, 2))
     send_beside((0, 3))
     send_ring((0, 1, 2, 3))
     for g in (0, 1):
@@ -327,6 +321,8 @@
             device_id=(y_peer[o], s), device_id_type=MESH)
         copy.start()
         to_y.append(copy)
+    send_across((3,))
+    hand_on((0,))
     for copy in to_y:
         copy.wait_recv()
     total = f2[y].reshape(48, 256)
@@ -398,7 +394,7 @@
         @pl.when(here)
         def _(k=k):
             for j in (0, 1):
-                for i in (1, 2):
+                for i in (0, 1, 2):
                     from_hand(k, j, i).wait_send()
 
     for k in (1, 2, 3):
@@ -422,7 +418,7 @@
         out_specs=(vmem, vmem),
         scratch_shapes=[
             pltpu.VMEM((4, 256, 256), BF16),
-            pltpu.VMEM((16, 256, 256), BF16),
+            pltpu.VMEM((4, 4, 256, 256), BF16),
             pltpu.VMEM((16, 256, 256), BF16),
             pltpu.VMEM((4, 256, 256), BF16),
             pltpu.VMEM((6, 256, 256), BF16),
@@ -430,7 +426,7 @@
             pltpu.VMEM((17, 256, 256), BF16),
             pltpu.VMEM((16, 256, 256), BF16),
             pltpu.VMEM((6, 4, 256, 256), BF16),
-            pltpu.VMEM((4, 256, 256), BF16),
+            pltpu.VMEM((6, 256, 256), BF16),
             pltpu.VMEM((6, 2, 128, 256), BF16),
             pltpu.VMEM((6, 128, 256), BF16),
             pltpu.VMEM((6, 4, 32, 256), BF16),
@@ -442,7 +438,7 @@
             pltpu.VMEM((32, 256), BF16),
             pltpu.VMEM((2, 8, 256), F32),
             pltpu.VMEM((2, 2, 8, 256), F32),
-            dma((7,)), dma((2,)), dma((2,)), dma((6, 4)), dma((6, 4)), dma((4,)), dma((4,)),
+            dma((7,)), dma((2,)), dma((2,)), dma((6, 4)), dma((6, 4)), dma((6,)), dma((6,)),
             dma((2,)), dma((2,)), dma((2, 3)), dma((2, 3)), dma((3,)), dma((3,)),
             dma((1,)), dma((1,)), dma((2, 2)), dma((2, 2)),
         ],
@@ -452,7 +448,7 @@
     )(
         charges, present_blocks, directions.reshape(4),
         wavefunction,
-        left_operators.reshape(16, 256, 256),
+        left_operators,
         right_operators.reshape(16, 256, 256),
         rotations,
     )

time: 51.3 us -> 48.7 us (0.949)
  the two profiles are of different devices: /device:TPU:6 before, /device:TPU:1 now
where the time goes in v4:
time: 48.7 us; the launch traced here: 48.6 us
  Pallas kernels  45.3 us (93%)
  local copies, waits for them, and re-layouts  2.62 us (5%)
  between operations  0.64 us (1%)
    pallas_call x1, Pallas kernels, body(): pl.pallas_call(kernel, out_shape=(pltpu.VMEM((4, 4, 256), F32), pltpu.VME...  45.3 us
    unnamed x2, local copies, waits for them, and re-layouts  2.62 us

profile of v4, /device:TPU:1, one launch (start us, length us, event | category | flops | bytes accessed | tf_op | source)
XLA Modules:
  0.0 48.6 jit_solution(10162557885555329151)
XLA Ops:
  0.6 45.3 %step.1 = (f32[4,4,256]{2,1,0:T(4,128)S(1)}, bf16[8,4,256,256]{3,2,1,0:T(8,128)(2,1)S(1)}) custom-call(s32[4]{0:T(128)} %chg.1, s32[4,4]{1,0:T(4,128)} %pres.1, s32[4]{0:T(128)} %bitcast.3, bf16[4,256,256]{2,1,0:T(8,128)(2,1)} %psi_h.1, bf16[4,4,256,256]{3,2,1,0:T(8,128)(2,1)} %left_h.1, bf16[16,256,256]{2,1,0:T(8,128)(2,1)} %bitcast.2, ...), custom_call_target="tpu_custom_call" | custom-call | tf_op jit(solution)/shard_map/step/pallas_call | solution.py:411
  46.0 0.6 %copy.11 = f32[4,4,256]{2,1,0:T(4,128)} copy(f32[4,4,256]{2,1,0:T(4,128)S(1)} %get-tuple-element.2) | data formatting | bytes 32768
  46.6 2.0 %copy.12 = bf16[8,4,256,256]{3,2,1,0:T(8,128)(2,1)} copy(bf16[8,4,256,256]{3,2,1,0:T(8,128)(2,1)S(1)} %get-tuple-element.3) | data formatting | bytes 8388608

commit v5 on v4

--- a/solution.py
+++ b/solution.py
@@ -9,6 +9,8 @@
 F32 = jnp.float32
 BF16 = jnp.bfloat16
 NT = (((1,), (1,)), ((), ()))
+MIDDLE = [(1, 0), (1, 1), (2, 0), (2, 1), (3, 0)]
+SIDE = [(0, 0), (0, 1)]
 
 
 def place(y, zh, x, c):
@@ -37,6 +39,10 @@
     hand_down = jnp.logical_and(x == 1, c == 1)
     via_up = place((y + zh) % 4, zh, 2, 0)
     via_down = place((y + 3 + zh) % 4, zh, 1, 1)
+    side_up = (x == 3) & (c == 0)
+    side_down = (x == 0) & (c == 1)
+    past_up = place((y + zh) % 4, zh, 3, 0)
+    past_down = place((y + 3 + zh) % 4, zh, 0, 1)
     late_up = place(y, 1 - zh, 2, 0)
     late_down = place(y, 1 - zh, 1, 1)
     from_up = place((y + 4 - zh) % 4, zh, 3, 1)
@@ -71,8 +77,10 @@
             for peer in peers:
                 pl.semaphore_signal(bar, inc=1, device_id=(peer, s), device_id_type=MESH)
 
-    greet(far_up, (via_up, late_down))
-    greet(far_down, (via_down, late_up))
+    greet(far_up, (via_up, late_down, past_up, place(y, 1 - zh, 0, 1)))
+    greet(far_down, (via_down, late_up, past_down, place(y, 1 - zh, 3, 0)))
+    greet(side_up, (from_up, onto_up))
+    greet(side_down, (from_down, onto_down))
     greet(hand_up, (from_up, onto_up))
     greet(hand_down, (from_down, onto_down))
 
@@ -134,7 +142,8 @@
         n, h = 2 * (k - 1) + j, 2 * i + j
         return pltpu.make_async_remote_copy(
             pay.at[n, i], hand.at[h], pay_s.at[n, i], hand_r.at[h],
-            device_id=({1: via_up, 2: via_down}[k], s), device_id_type=MESH)
+            device_id=((
+                {1: past_up, 2: past_down} if (i, j) in SIDE else {1: via_up, 2: via_down})[k], s), device_id_type=MESH)
 
     def from_hand(k, j, i):
         n, h = 2 * (k - 1) + j, 2 * i + j
@@ -148,7 +157,7 @@
             def _(k=k):
                 for i in sectors:
                     for j in (0, 1):
-                        (to_hand if i in (0, 1, 2) else moved)(k, j, i).start()
+                        (to_hand if (i, j) in SIDE + MIDDLE else moved)(k, j, i).start()
 
     def send_beside(sectors):
         for k, here in ((1, c == 0), (2, c == 1)):
@@ -171,14 +180,13 @@
             for j in (0, 1):
                 moved(3, j, i).start()
 
-    def hand_on(sectors):
-        for k, here in ((1, hand_up), (2, hand_down)):
+    def hand_on(blocks, ups, downs):
+        for k, here in ((1, ups), (2, downs)):
             @pl.when(here)
             def _(k=k):
-                for i in sectors:
-                    for j in (0, 1):
-                        to_hand(k, j, i).wait_recv()
-                        from_hand(k, j, i).start()
+                for i, j in blocks:
+                    to_hand(k, j, i).wait_recv()
+                    from_hand(k, j, i).start()
 
     def renormed(p, i):
         w = pres[p, i].astype(F32)
@@ -204,8 +212,9 @@
 
     lax.fori_loop(1, 3, inner, 0)
     sides = jnp.where(s > 0, 2, 0) + jnp.where(s < 3, 2, 0)
-    corner = far_up | far_down | hand_up | hand_down
-    pl.semaphore_wait(bar, 10 + sides + jnp.where(corner, 2, 0))
+    far = far_up | far_down
+    helps = hand_up | hand_down | side_up | side_down
+    pl.semaphore_wait(bar, 10 + sides + jnp.where(far, 4, 0) + jnp.where(helps, 2, 0))
 
     @pl.when(s < 3)
     def _():
@@ -295,7 +304,7 @@
         lax.fori_loop(3 * g, 3 * g + 3, core_sum, 0)
         for o in range(3):
             to_x(g, o).start()
-    hand_on((1, 2))
+    hand_on([b for b in MIDDLE if b[0] in (1, 2)], hand_up, hand_down)
     send_beside((0, 3))
     send_ring((0, 1, 2, 3))
     for g in (0, 1):
@@ -322,7 +331,8 @@
         copy.start()
         to_y.append(copy)
     send_across((3,))
-    hand_on((0,))
+    hand_on(SIDE, side_up, side_down)
+    hand_on([b for b in MIDDLE if b[0] in (0, 3)], hand_up, hand_down)
     for copy in to_y:
         copy.wait_recv()
     total = f2[y].reshape(48, 256)
@@ -390,12 +400,13 @@
         edge(0, 1).wait_send()
         to_below().wait_send()
 
-    for k, here in ((1, hand_up), (2, hand_down)):
+    for k, here, blocks in (
+        (1, hand_up, MIDDLE), (2, hand_down, MIDDLE), (1, side_up, SIDE), (2, side_down, SIDE),
+    ):
         @pl.when(here)
-        def _(k=k):
-            for j in (0, 1):
-                for i in (0, 1, 2):
-                    from_hand(k, j, i).wait_send()
+        def _(k=k, blocks=blocks):
+            for i, j in blocks:
+                from_hand(k, j, i).wait_send()
 
     for k in (1, 2, 3):
         for j in (0, 1):
@@ -426,7 +437,7 @@
             pltpu.VMEM((17, 256, 256), BF16),
             pltpu.VMEM((16, 256, 256), BF16),
             pltpu.VMEM((6, 4, 256, 256), BF16),
-            pltpu.VMEM((6, 256, 256), BF16),
+            pltpu.VMEM((8, 256, 256), BF16),
             pltpu.VMEM((6, 2, 128, 256), BF16),
             pltpu.VMEM((6, 128, 256), BF16),
             pltpu.VMEM((6, 4, 32, 256), BF16),
@@ -438,7 +449,7 @@
             pltpu.VMEM((32, 256), BF16),
             pltpu.VMEM((2, 8, 256), F32),
             pltpu.VMEM((2, 2, 8, 256), F32),
-            dma((7,)), dma((2,)), dma((2,)), dma((6, 4)), dma((6, 4)), dma((6,)), dma((6,)),
+            dma((7,)), dma((2,)), dma((2,)), dma((6, 4)), dma((6, 4)), dma((8,)), dma((8,)),
             dma((2,)), dma((2,)), dma((2, 3)), dma((2, 3)), dma((3,)), dma((3,)),
             dma((1,)), dma((1,)), dma((2, 2)), dma((2, 2)),
         ],

time: 48.7 us -> 47.3 us (0.971)
  the two profiles are of different devices: /device:TPU:1 before, /device:TPU:6 now
where the time goes in v5:
time: 47.3 us; the launch traced here: 47.2 us
  Pallas kernels  43.9 us (93%)
  local copies, waits for them, and re-layouts  2.62 us (6%)
  between operations  0.64 us (1%)
    pallas_call x1, Pallas kernels, body(): pl.pallas_call(kernel, out_shape=(pltpu.VMEM((4, 4, 256), F32), pltpu.VME...  43.9 us
    unnamed x2, local copies, waits for them, and re-layouts  2.62 us

profile of v5, /device:TPU:6, one launch (start us, length us, event | category | flops | bytes accessed | tf_op | source)
XLA Modules:
  0.0 47.2 jit_solution(1064187136690051342)
XLA Ops:
  0.6 43.9 %step.1 = (f32[4,4,256]{2,1,0:T(4,128)S(1)}, bf16[8,4,256,256]{3,2,1,0:T(8,128)(2,1)S(1)}) custom-call(s32[4]{0:T(128)} %chg.1, s32[4,4]{1,0:T(4,128)} %pres.1, s32[4]{0:T(128)} %bitcast.3, bf16[4,256,256]{2,1,0:T(8,128)(2,1)} %psi_h.1, bf16[4,4,256,256]{3,2,1,0:T(8,128)(2,1)} %left_h.1, bf16[16,256,256]{2,1,0:T(8,128)(2,1)} %bitcast.2, ...), custom_call_target="tpu_custom_call" | custom-call | tf_op jit(solution)/shard_map/step/pallas_call | solution.py:422
  44.5 0.6 %copy.11 = f32[4,4,256]{2,1,0:T(4,128)} copy(f32[4,4,256]{2,1,0:T(4,128)S(1)} %get-tuple-element.2) | data formatting | bytes 32768
  45.1 2.0 %copy.12 = bf16[8,4,256,256]{3,2,1,0:T(8,128)(2,1)} copy(bf16[8,4,256,256]{3,2,1,0:T(8,128)(2,1)S(1)} %get-tuple-element.3) | data formatting | bytes 8388608

commit v6 on v5

--- a/solution.py
+++ b/solution.py
@@ -246,6 +246,11 @@
     natural = ((row // 8) % 4) * 64 + ((row // 4) % 2) * 32 + ((row // 32) % 4) * 8 + (row // 128) * 4 + row % 4
     order = (col == natural).astype(BF16)
 
+    def put(e, total):
+        placed = jnp.dot(order, total.astype(BF16), preferred_element_type=F32).astype(BF16)
+        part[e, 0] = placed[:128]
+        part[e, 1] = placed[128:]
+
     def target_sum(e, _):
         total = jnp.zeros((256, 256), F32)
         for p in range(4):
@@ -254,10 +259,18 @@
             clipped = jnp.clip(src, 0, 3)
             lhs = half[jnp.where(inside, 4 * clipped + p, 16)]
             total = total + lax.dot_general(lhs, right[4 * p + clipped], NT, preferred_element_type=F32)
-        placed = jnp.dot(order, total.astype(BF16), preferred_element_type=F32).astype(BF16)
-        part[e, 0] = placed[:128]
-        part[e, 1] = placed[128:]
-        return 0
+        put(e, total)
+        return 0
+
+    outside = [jnp.zeros((256, 256), F32), jnp.zeros((256, 256), F32)]
+    for p in range(4):
+        low, high = chg[p] == -1, chg[p] == 1
+        lhs = half[jnp.where(low, p, jnp.where(high, 12 + p, 16))]
+        both = lax.dot_general(lhs, right[4 * p + jnp.where(low, 0, 3)], NT, preferred_element_type=F32)
+        outside[0] = outside[0] + both * low.astype(F32)
+        outside[1] = outside[1] + both * high.astype(F32)
+    put(0, outside[0])
+    put(5, outside[1])
 
     def to_core(g):
         some = pl.ds(3 * g, 3)
@@ -271,7 +284,7 @@
             device_id=(x_peer[o], s), device_id_type=MESH)
 
     for g in (0, 1):
-        lax.fori_loop(3 * g, 3 * g + 3, target_sum, 0)
+        lax.fori_loop(1 + 2 * g, 3 + 2 * g, target_sum, 0)
         to_core(g).start()
 
     for i in (0, 3):

time: 47.3 us -> 47.2 us (level)
  no operation moved by 1% of the time
where the time goes in v6:
time: 47.2 us; the launch traced here: 47 us
  Pallas kernels  43.7 us (93%)
  local copies, waits for them, and re-layouts  2.62 us (6%)
  between operations  0.64 us (1%)
    pallas_call x1, Pallas kernels, body(): pl.pallas_call(kernel, out_shape=(pltpu.VMEM((4, 4, 256), F32), pltpu.VME...  43.7 us
    unnamed x2, local copies, waits for them, and re-layouts  2.62 us

profile of v6, /device:TPU:6, one launch (start us, length us, event | category | flops | bytes accessed | tf_op | source)
XLA Modules:
  0.0 47.0 jit_solution(3832944005196450079)
XLA Ops:
  0.6 43.7 %step.1 = (f32[4,4,256]{2,1,0:T(4,128)S(1)}, bf16[8,4,256,256]{3,2,1,0:T(8,128)(2,1)S(1)}) custom-call(s32[4]{0:T(128)} %chg.1, s32[4,4]{1,0:T(4,128)} %pres.1, s32[4]{0:T(128)} %bitcast.3, bf16[4,256,256]{2,1,0:T(8,128)(2,1)} %psi_h.1, bf16[4,4,256,256]{3,2,1,0:T(8,128)(2,1)} %left_h.1, bf16[16,256,256]{2,1,0:T(8,128)(2,1)} %bitcast.2, ...), custom_call_target="tpu_custom_call" | custom-call | tf_op jit(solution)/shard_map/step/pallas_call | solution.py:435
  44.4 0.6 %copy.11 = f32[4,4,256]{2,1,0:T(4,128)} copy(f32[4,4,256]{2,1,0:T(4,128)S(1)} %get-tuple-element.2) | data formatting | bytes 32768
  45.0 2.0 %copy.12 = bf16[8,4,256,256]{3,2,1,0:T(8,128)(2,1)} copy(bf16[8,4,256,256]{3,2,1,0:T(8,128)(2,1)S(1)} %get-tuple-element.3) | data formatting | bytes 8388608
